TPU v7x, 32 devices: a whole 2x2x4 slice. The times are simulated.
32 devices in a mesh: patch: 2 (over y), visit: 4 (over z), tile: 4 (over x, core).
Axes of the slice: x: 2, y: 2, z: 4, core: 2. Of those that a mesh axis runs over, the one named last changes fastest.
Arguments:
- exposure: float32 [16, 256, 4096], P('visit', ('patch', 'tile')), parts along dimension 1, may hold values from -12 to 12
- variance: float32 [16, 256, 4096], P('visit', ('patch', 'tile')), parts along dimension 1, may hold values from 0.25 to 4
- usable: int32 [16, 256, 4096], P('visit', ('patch', 'tile')), parts along dimension 1, may hold values from 0 to 1, as said below
- basis_width: float32 [32, 3], P(('patch', 'visit')), parts along dimension 0, may hold values from 0.8 to 3.5
- spatial_coef: float32 [32, 3, 6], P(('patch', 'visit')), parts along dimension 0, may hold values from -0.6 to 1.4
Outputs:
- coadd: float32 [256, 4096], P(('patch', 'tile')), parts along dimension 0
There are 2 independent parts, one for each index of `patch`. A program takes and returns all parts, laid end to end along the dimension named above; each array names one. Nothing has to cross between parts.
Inputs may be any that keep to these rules, and one draw needn't show every extreme that they name: 1 marks a usable sample; at every pixel at least 5 of the 16 visits are usable.
All inputs are finite; a program needn't handle non-finite values.
Results may differ from a plain program's by a relative error of at most 0.0003.
Values sent between devices are 32-bit elements; how exact they have to be, the bound alone decides.
No kernel may reach another device: no remote copies, remote signals or barrier semaphores. Data moves between devices by JAX's collectives and lax.ppermute only.
A program may use at most 128 MiB of HBM per device.

v0:
```python
import jax
import jax.numpy as jnp
from jax import lax
from jax.sharding import PartitionSpec as P

KHALF = 15
BASES = 3


big_value = 1e30


def with_halo(cells, sides, width):
    for axis, dim in sides:
        count = lax.axis_size(axis)
        ends = count - 1
        head = lax.slice_in_dim(cells, 0, width, axis=dim)
        tail = lax.slice_in_dim(cells, cells.shape[dim] - width, cells.shape[dim], axis=dim)
        cells = jnp.concatenate(
            [
                lax.ppermute(tail, axis, [(i, (i + 1) % count) for i in range(ends)]),
                cells,
                lax.ppermute(head, axis, [((i + 1) % count, i) for i in range(ends)]),
            ],
            axis=dim,
        )
    return cells


def combined_all(array, axis, combine):
    everything = jax.tree.map(lambda part: lax.all_gather(part, axis), array)
    initial = jax.tree.map(lambda part: part[0], everything)

    def step(k, so_far):
        return combine(so_far, jax.tree.map(lambda part: part[k], everything))

    return lax.fori_loop(1, lax.axis_size(axis), step, initial)


def basis_profile(offsets, width, basis_id):
    profile = jnp.exp(-offsets * offsets / (2.0 * width * width))
    if basis_id > 0:
        profile = profile * (offsets / width) ** (2 * basis_id)
    return profile


def merge_records(first, second):
    smallest = jnp.minimum(first[0], second[0])
    second_low = jnp.minimum(jnp.minimum(first[1], second[1]), jnp.maximum(first[0], second[0]))
    third_low = jnp.minimum(
        jnp.minimum(first[2], second[2]),
        jnp.minimum(jnp.maximum(first[0], second[1]), jnp.maximum(first[1], second[0])),
    )
    largest = jnp.maximum(first[3], second[3])
    second_high = jnp.maximum(jnp.maximum(first[4], second[4]), jnp.minimum(first[3], second[3]))
    third_high = jnp.maximum(
        jnp.maximum(first[5], second[5]),
        jnp.maximum(jnp.minimum(first[3], second[4]), jnp.minimum(first[4], second[3])),
    )
    return (smallest, second_low, third_low, largest, second_high, third_high)


def band_matrices(offsets_grid, basis_width, totals):
    inside = (jnp.abs(offsets_grid) <= KHALF).astype(jnp.float32)
    matrices = []
    for basis_id in range(BASES):
        widths = basis_width[:, basis_id][:, None, None]
        profile = basis_profile(offsets_grid[None], widths, basis_id)
        matrices.append(profile * inside[None] / totals[:, basis_id][:, None, None])
    return jnp.stack(matrices, axis=1)


def per_device(exposure, variance, usable, basis_width, spatial_coef):
    visits_here, row_count, col_count = exposure.shape
    offsets = jnp.arange(-KHALF, KHALF + 1).astype(jnp.float32)
    totals = jnp.stack(
        [
            jnp.sum(
                basis_profile(offsets[None, :], basis_width[:, basis_id : basis_id + 1], basis_id),
                axis=1,
            )
            for basis_id in range(BASES)
        ],
        axis=1,
    )
    extended = with_halo(exposure, (("tile", 1),), KHALF)
    out_rows = jnp.arange(row_count)[:, None]
    in_rows = jnp.arange(row_count + 2 * KHALF)[None, :]
    vertical_offsets = (in_rows - out_rows - KHALF).astype(jnp.float32)
    vertical_mats = band_matrices(vertical_offsets, basis_width, totals)
    vertical = jnp.einsum(
        "vbij,vjc->vbic", vertical_mats, extended, precision=lax.Precision.HIGHEST
    )
    in_cols = jnp.arange(384)[:, None]
    out_cols = jnp.arange(128)[None, :]
    across_offsets = (in_cols - 128 - out_cols).astype(jnp.float32)
    across_mats = band_matrices(across_offsets, basis_width, totals)
    blocks = col_count // 128
    centre = vertical.reshape(visits_here, BASES, row_count, blocks, 128)
    zero_block = jnp.zeros_like(centre[:, :, :, :1])
    left_side = jnp.concatenate([zero_block, centre[:, :, :, :-1]], axis=3)
    right_side = jnp.concatenate([centre[:, :, :, 1:], zero_block], axis=3)
    stacked = jnp.concatenate([left_side, centre, right_side], axis=4)
    smoothed = jnp.einsum(
        "vbrnk,vbkj->vbrnj", stacked, across_mats, precision=lax.Precision.HIGHEST
    )
    smoothed = smoothed.reshape(visits_here, BASES, row_count, col_count)
    total_rows = row_count * lax.axis_size("tile")
    row_global = (lax.axis_index("tile") * row_count + jnp.arange(row_count)).astype(jnp.float32)
    row_pos = 2.0 * row_global / (total_rows - 1) - 1.0
    col_pos = 2.0 * jnp.arange(col_count).astype(jnp.float32) / (col_count - 1) - 1.0
    ycoord = jnp.broadcast_to(row_pos[:, None], (row_count, col_count))
    xcoord = jnp.broadcast_to(col_pos[None, :], (row_count, col_count))
    poly_terms = jnp.stack(
        [
            jnp.ones((row_count, col_count), jnp.float32),
            xcoord,
            ycoord,
            xcoord * xcoord,
            xcoord * ycoord,
            ycoord * ycoord,
        ]
    )
    factor = jnp.einsum("vbk,krc->vbrc", spatial_coef, poly_terms, precision=lax.Precision.HIGHEST)
    matched = jnp.sum(factor * smoothed, axis=1)
    valid = usable > 0
    low_side = jnp.where(valid, matched, big_value)
    high_side = jnp.where(valid, matched, -big_value)
    big_plane = jnp.full((row_count, col_count), big_value, jnp.float32)
    records = (big_plane, big_plane, big_plane, -big_plane, -big_plane, -big_plane)
    for visit_id in range(visits_here):
        single = (
            low_side[visit_id],
            big_plane,
            big_plane,
            high_side[visit_id],
            -big_plane,
            -big_plane,
        )
        records = merge_records(records, single)
    merged = combined_all(records, "visit", merge_records)
    lower = merged[2]
    upper = merged[5]
    weight = jnp.where(valid, 1.0 / variance, 0.0)
    numer = jnp.sum(weight * jnp.clip(matched, lower, upper), axis=0)
    denom = jnp.sum(weight, axis=0)
    numer_all, denom_all = lax.psum((numer, denom), "visit")
    return numer_all / denom_all


def solution(mesh):
    in_specs = (
        P("visit", ("patch", "tile"), None),
        P("visit", ("patch", "tile"), None),
        P("visit", ("patch", "tile"), None),
        P(("patch", "visit"), None),
        P(("patch", "visit"), None, None),
    )
    out_specs = P(("patch", "tile"), None)
    return jax.shard_map(
        per_device, mesh=mesh, in_specs=in_specs, out_specs=out_specs, check_vma=False
    )
```

profile of v0, /device:TPU:0, one launch (start us, length us, event | category | flops | bytes accessed | tf_op | source)
XLA Modules:
  0.0 456.5 jit_solution(1731907902424152540)
XLA Ops:
  6.5 1.7 fusion.56
  8.3 1.6 copy.46
  9.9 3.3 collective-permute-start
  13.3 1.6 copy.47
  14.8 1.3 collective-permute-start.1
  16.1 0.6 add_convert_fusion
  16.8 0.6 fusion.41
  17.4 0.6 negate_multiply_fusion.1
  18.2 0.8 subtract_convert_fusion
  19.8 0.5 multiply_multiply_fusion.3
  20.9 0.8 fusion.48
  23.8 8.3 %stack.24 = f32[6,32,4096]{2,0,1:T(8,128)} concatenate(f32[1,32,4096]{2,0,1:T(1,128)S(1)} %stack_broadcast_in_dim.15, f32[1,32,4096]{2,0,1:T(1,128)S(1)} %stack_broadcast_in_dim.16, f32[1,32,4096]{2,0,1:T(1,128)S(1)} %stack_broadcast_in_dim.17, f32[1,32,4096]{2,0,1:T(1,128)S(1)} %stack.10, f32[1,32,4096]{2,0,1:T(1,128)S(1)} %broadcast_multiply_fusion, f32[1,32,4096]{2,0,1:T(1,128)S(1)} %stack.11), dimensions={0} | concatenate | bytes 6291456 | tf_op jit(solution)/shard_map/stack | solution.py:114
  32.1 0.9 fusion.38
  33.0 2.8 fusion.22
  35.8 1.9 copy.35
  37.7 1.8 copy.36
  39.5 5.2 %fusion.9 = f32[4,3,32,4096]{3,2,1,0:T(8,128)S(1)} fusion(f32[4,15,4096]{2,1,0:T(8,128)S(1)} %copy.36, f32[4,32,4096]{2,1,0:T(8,128)S(1)} %copy-done.1, f32[4,15,4096]{2,1,0:T(8,128)S(1)} %copy.35, f32[4,1,32,62]{3,2,1,0:T(8,128)S(1)} %get-tuple-element.382, f32[4,1,32,62]{3,2,1,0:T(8,128)S(1)} %get-tuple-element.381, ...), kind=kOutput, calls=%fused_computation.27 | convolution fusion | flops 1172290048 | bytes 10449920 | tf_op jit(solution)/shard_map/vbij,vjc->vbic/dot_general | solution.py:91
  44.8 1.3 copy.48
  46.1 6.3 %fusion.55 = (f32[4,3,32,31,128]{4,3,2,1,0:T(8,128)}, f32[4,3,32,31,128]{4,3,2,1,0:T(8,128)}) fusion(f32[4,3,32,32,128]{4,3,2,1,0:T(8,128)S(1)} %bitcast.90), kind=kLoop, calls=%fused_computation.139 | loop fusion | bytes 24379392 | tf_op jit(solution)/shard_map/slice | solution.py:101
  52.4 20.0 %fusion.6 = f32[4,3,32,32,128]{4,3,0,1,2:T(8,128)} fusion(f32[4,3,32,31,128]{4,3,2,1,0:T(8,128)} %get-tuple-element.371, f32[4,3,32,31,128]{4,3,2,1,0:T(8,128)} %get-tuple-element.370, f32[4,3,32,32,128]{4,3,2,1,0:T(8,128)S(1)} %bitcast.91, f32[4,1,384,128]{3,2,1,0:T(8,128)} %get-tuple-element.379, f32[4,1,384,128]{3,2,1,0:T(8,128)} %get-tuple-element.378, ...), kind=kOutput, calls=%fused_computation.22 | convolution fusion | flops 7277248512 | bytes 27131904 | tf_op jit(solution)/shard_map/vbrnk,vbkj->vbrnj/dot_general | solution.py:104
  72.4 7.6 %reshape.342 = f32[4,3,32,4096]{3,0,1,2:T(4,128)} reshape(f32[4,3,32,32,128]{4,3,0,1,2:T(8,128)} %fusion.6) | data formatting | bytes 12582912 | tf_op jit(solution)/shard_map/reshape | solution.py:107
  80.1 14.7 %fusion.8 = f32[4,32,4096]{2,0,1:T(4,128)S(1)} fusion(f32[4,3,32,4096]{3,0,1,2:T(4,128)} %reshape.342, f32[6,32,4096]{2,0,1:T(8,128)} %stack.24, f32[4,3,6]{2,0,1:T(4,128)S(1)} %copy-done), kind=kOutput, calls=%fused_computation.25 | convolution fusion | flops 115867648 | bytes 11534624 | tf_op jit(solution)/shard_map/vbk,krc->vbrc/dot_general | solution.py:124
  94.8 1.6 copy_select_fusion
  96.4 1.2 maximum_maximum_fusion
  97.6 1.2 minimum_maximum_fusion
  98.9 0.7 all-gather.13.cloned.1.call-update
  99.7 1.5 copy_select_fusion.1
  101.1 1.2 minimum_minimum_fusion
  102.4 1.2 maximum_minimum_fusion
  105.4 42.9 %all-gather.15.cloned.1.call-done = f32[4,32,4096]{2,1,0:T(8,128)} async-done(((f32[1,32,4096]{2,1,0:T(8,128)}), f32[4,32,4096]{2,1,0:T(8,128)}) %all-gather.15.cloned.1.call-update) | async-done | bytes 2097168 | tf_op jit(solution)/shard_map/all_gather | solution.py:31
  148.3 1.9 slice_bitcast_fusion.1
  150.2 44.2 %all-gather.13.cloned.1.call-done = f32[4,32,4096]{2,1,0:T(8,128)} async-done(((f32[1,32,4096]{2,1,0:T(8,128)}), f32[4,32,4096]{2,1,0:T(8,128)}) %all-gather.13.cloned.1.call-update) | async-done | bytes 2097168 | tf_op jit(solution)/shard_map/all_gather | solution.py:31
  194.4 1.8 slice_bitcast_fusion.2
  196.2 44.2 %all-gather.9.cloned.1.call-done = f32[4,32,4096]{2,1,0:T(8,128)} async-done(((f32[1,32,4096]{2,1,0:T(8,128)}), f32[4,32,4096]{2,1,0:T(8,128)}) %all-gather.9.cloned.1.call-update) | async-done | bytes 2097168 | tf_op jit(solution)/shard_map/all_gather | solution.py:31
  240.5 1.9 slice_bitcast_fusion.4
  242.3 44.0 %all-gather.7.cloned.1.call-done = f32[4,32,4096]{2,1,0:T(8,128)} async-done(((f32[1,32,4096]{2,1,0:T(8,128)}), f32[4,32,4096]{2,1,0:T(8,128)}) %all-gather.7.cloned.1.call-update) | async-done | bytes 2097168 | tf_op jit(solution)/shard_map/all_gather | solution.py:31
  286.4 1.9 slice_bitcast_fusion.5
  288.2 44.0 %all-gather.11.cloned.1.call-done = f32[4,32,4096]{2,1,0:T(8,128)} async-done(((f32[1,32,4096]{2,1,0:T(8,128)}), f32[4,32,4096]{2,1,0:T(8,128)}) %all-gather.11.cloned.1.call-update) | async-done | bytes 2097168 | tf_op jit(solution)/shard_map/all_gather | solution.py:31
  332.3 1.1 slice_bitcast_fusion.3
  333.4 44.8 %all-gather.17.cloned.1.call-done = f32[4,32,4096]{2,1,0:T(8,128)} async-done(((f32[1,32,4096]{2,1,0:T(8,128)}), f32[4,32,4096]{2,1,0:T(8,128)}) %all-gather.17.cloned.1.call-update) | async-done | bytes 2097168 | tf_op jit(solution)/shard_map/all_gather | solution.py:31
  378.2 1.1 slice_bitcast_fusion
  379.3 12.9 %while.25 = (s32[]{:T(128)}, f32[32,4096]{1,0:T(8,128)}, f32[32,4096]{1,0:T(8,128)}, f32[32,4096]{1,0:T(8,128)S(1)}, f32[32,4096]{1,0:T(8,128)}, /*index=5*/f32[...) while((s32[]{:T(128)}, f32[32,4096]{1,0:T(8,128)}, ...), condition=%wide.region_5.6_spmd, body=%wide.region_4.5_spmd.sunk | while | flops 2359301 | bytes 9437379 | solution.py:37
  379.3 4.3 fusion.58
  383.6 4.3 fusion.58
  387.9 4.3 fusion.58
  392.2 4.5 fusion.25
  396.6 50.9 %all-reduce.5.cloned.1.call-done = (f32[32,4096]{1,0:T(8,128)}, f32[32,4096]{1,0:T(8,128)}) async-done(((f32[32,4096]{1,0:T(8,128)}, f32[32,4096]{1,0:T(8,128)}), (f32[32,4096]{1,0:T(8,128)}, f32[32,4096]{1,0:T(8,128)})) %all-reduce.5.cloned.1.call-update) | async-done | bytes 1048592 | tf_op jit(solution)/shard_map/psum | solution.py:147
  447.6 2.1 div.443
  (41 shorter events, 5.5 us)
Async XLA Ops:
  6.5 73.5 %copy-start = (f32[4,3,6]{2,0,1:T(4,128)S(1)}, f32[4,3,6]{2,0,1:T(4,128)}, u32[]{:S(2)}) copy-start(f32[4,3,6]{2,0,1:T(4,128)} %param.11) | copy-start | bytes 868
  6.5 141.8 %all-gather.15.cloned.1.call-start = ((), (), s32[]{:S(2)}) async-start(), calls=%async_computation.4 | async-start | bytes 2621440 | tf_op jit(solution)/shard_map/all_gather | solution.py:31
  8.3 10.7 %copy-start.4 = (f32[4,3]{1,0:T(4,128)S(1)}, f32[4,3]{1,0:T(4,128)}, u32[]{:S(2)}) copy-start(f32[4,3]{1,0:T(4,128)} %param.10) | copy-start | bytes 148
  9.9 25.9 %collective-permute-start = (f32[4,15,4096]{2,0,1:T(4,128)}, f32[4,15,4096]{2,0,1:T(4,128)}, u32[]{:S(2)}, u32[]{:S(2)}) collective-permute-start(f32[4,15,4096]{2,0,1:T(4,128)} %copy.46), channel_id=1, source_target_pairs={{0,1},{1,2},{2,3},{4,5},{5,6},{6,7},{8,9},{9,10},{10,11},{12,13},{... | collective-permute-start | bytes 2949128 | tf_op jit(solution)/shard_map/ppermute | solution.py:21
  14.8 22.9 %collective-permute-start.1 = (f32[4,15,4096]{2,0,1:T(4,128)}, f32[4,15,4096]{2,0,1:T(4,128)}, u32[]{:S(2)}, u32[]{:S(2)}) collective-permute-start(f32[4,15,4096]{2,0,1:T(4,128)} %copy.47), channel_id=1, source_target_pairs={{1,0},{2,1},{3,2},{5,4},{6,5},{7,6},{9,8},{10,9},{11,10},{13,12},{... | collective-permute-start | bytes 2949128 | tf_op jit(solution)/shard_map/ppermute | solution.py:23
  35.8 3.7 copy-start.1
  80.1 14.8 %copy-start.3 = (s32[4,32,4096]{2,1,0:T(8,128)S(1)}, s32[4,32,4096]{2,1,0:T(8,128)}, u32[]{:S(2)}) copy-start(s32[4,32,4096]{2,1,0:T(8,128)} %param.9) | copy-start | bytes 6291460
  96.4 3.3 copy-start.2
  98.9 95.5 %all-gather.13.cloned.1.call-start = ((), (), s32[]{:S(2)}) async-start(), calls=%async_computation.3 | async-start | bytes 2621440 | tf_op jit(solution)/shard_map/all_gather | solution.py:31
  99.6 140.8 %all-gather.9.cloned.1.call-start = ((), (), s32[]{:S(2)}) async-start(), calls=%async_computation.1 | async-start | bytes 2621440 | tf_op jit(solution)/shard_map/all_gather | solution.py:31
  103.6 182.8 %all-gather.7.cloned.1.call-start = ((), (), s32[]{:S(2)}) async-start(), calls=%async_computation | async-start | bytes 2621440 | tf_op jit(solution)/shard_map/all_gather | solution.py:31
  104.2 228.1 %all-gather.11.cloned.1.call-start = ((), (), s32[]{:S(2)}) async-start(), calls=%async_computation.2 | async-start | bytes 2621440 | tf_op jit(solution)/shard_map/all_gather | solution.py:31
  104.8 273.4 %all-gather.17.cloned.1.call-start = ((), (), s32[]{:S(2)}) async-start(), calls=%async_computation.5 | async-start | bytes 2621440 | tf_op jit(solution)/shard_map/all_gather | solution.py:31
  105.4 342.2 %all-reduce.5.cloned.1.call-start = ((), (), s32[]{:S(2)}) async-start(), calls=%async_computation.6 | async-start | bytes 2097152 | tf_op jit(solution)/shard_map/psum | solution.py:147
Sparse Core Ops, SparseCore 0:
  99.0 49.2 all-gather.14
  149.9 44.4 all-gather.12
  196.0 44.4 all-gather.8
  241.9 44.4 all-gather.6
  287.8 44.4 all-gather.10
  333.7 44.4 all-gather.16
  396.8 50.7 all-reduce.4
where the time goes:
time: 457 us; the launch traced here: 456 us
  waiting for transfers between devices  317 us (69%)
  local copies, waits for them, and re-layouts  43.9 us (10%)
  matrix products  40 us (9%)
  other arithmetic  36.5 us (8%)
  between operations  13.7 us (3%)
  starting transfers between devices  4.87 us (1%)
    all_gather x6, waiting for transfers between devices, combined_all(): everything = jax.tree.map(lambda part: lax.all_gather(part, axis), array)  264 us
    psum x1, waiting for transfers between devices, per_device(): numer_all, denom_all = lax.psum((numer, denom), 'visit')  50.9 us
    dot_general x1, matrix products, per_device(): jnp.einsum('vbrnk,vbkj->vbrnj', stacked, across_mats, precision=lax.Preci...  20 us
    dot_general x1, matrix products, per_device(): jnp.einsum('vbk,krc->vbrc', spatial_coef, poly_terms, precision=lax.Preci...  14.7 us
    max x4, other arithmetic, merge_records(): jnp.maximum(jnp.maximum(first[5], second[5]), jnp.maximum(jnp.minimum(fir...  14.1 us
    another operation x6, local copies, waits for them, and re-layouts, per_device(): jnp.stack([jnp.ones((row_count, col_count), jnp.float32), xcoord, ycoord,...  10.4 us
    squeeze x6, local copies, waits for them, and re-layouts, combined_all(): initial = jax.tree.map(lambda part: part[0], everything)  9.62 us
  transfers between devices with their start and end apart: 9, of which 7 were waited for; matrix products, arithmetic and copies ran while one was open for 8% of the time, Pallas kernels for 0%

commit v1 on v0

v1 whole, which is shorter than its diff:
```python
import functools
import jax
import jax.numpy as jnp
from jax import lax
from jax.experimental import pallas as pl
from jax.experimental.pallas import tpu as pltpu
from jax.sharding import PartitionSpec as P

KHALF = 15
BASES = 3
HALO = 16
LANES = 128
big_value = 1e30


def profile_of(offsets, width, basis_id):
    ratio = (offsets / width) * (offsets / width)
    profile = jnp.exp(-0.5 * ratio)
    for _ in range(basis_id):
        profile = profile * ratio
    return jnp.where(jnp.abs(offsets) <= KHALF, profile, 0.0)


def split(values):
    high = values.astype(jnp.bfloat16)
    low = (values - high.astype(jnp.float32)).astype(jnp.bfloat16)
    return high, low


def prep_kernel(rows, width_ref, down_ref, across_ref):
    visit = pl.program_id(0)
    depth = rows + 2 * HALO
    tap = lax.broadcasted_iota(jnp.int32, (8, LANES), 1) - KHALF
    first = lax.broadcasted_iota(jnp.int32, (8, LANES), 0) == 0
    for basis_id in range(BASES):
        width = jnp.full((1, 1), width_ref[visit, basis_id], jnp.float32)
        raw = profile_of(tap.astype(jnp.float32), width, basis_id)
        total = jnp.sum(jnp.where(first, raw, 0.0), axis=(0, 1), keepdims=True)
        inverse = 1.0 / total
        in_row = lax.broadcasted_iota(jnp.int32, (rows, depth), 1)
        out_row = lax.broadcasted_iota(jnp.int32, (rows, depth), 0)
        offsets = (in_row - out_row - HALO).astype(jnp.float32)
        high, low = split(profile_of(offsets, width, basis_id) * inverse)
        here = pl.ds(basis_id * rows, rows)
        down_ref[0, here, :] = jnp.concatenate([high, low, high], axis=1)
        in_col = lax.broadcasted_iota(jnp.int32, (3 * LANES, LANES), 0)
        out_col = lax.broadcasted_iota(jnp.int32, (3 * LANES, LANES), 1)
        offsets = (in_col - out_col - LANES).astype(jnp.float32)
        high, low = split(profile_of(offsets, width, basis_id) * inverse)
        across_ref[0, basis_id, :, 0:LANES] = high
        across_ref[0, basis_id, :, LANES : 2 * LANES] = low


def prep(basis_width, rows):
    visits = basis_width.shape[0]
    depth = rows + 2 * HALO
    return pl.pallas_call(
        functools.partial(prep_kernel, rows),
        grid=(visits,),
        in_specs=[pl.BlockSpec(memory_space=pltpu.SMEM)],
        out_specs=[
            pl.BlockSpec((1, BASES * rows, 3 * depth), lambda v: (v, 0, 0)),
            pl.BlockSpec((1, BASES, 3 * LANES, 2 * LANES), lambda v: (v, 0, 0, 0)),
        ],
        out_shape=[
            jax.ShapeDtypeStruct((visits, BASES * rows, 3 * depth), jnp.bfloat16),
            jax.ShapeDtypeStruct((visits, BASES, 3 * LANES, 2 * LANES), jnp.bfloat16),
        ],
        name="band_matrices",
    )(basis_width)


def match_kernel(
    total_rows, total_cols, where_ref,
    mid, mid_l, mid_r, up, up_l, up_r, dn, dn_l, dn_r,
    variance, usable, down, across, coef, out, stacked,
):
    visit = pl.program_id(0)
    block_id = where_ref[0]
    tile_id = where_ref[1]
    rows, cols = mid.shape[1], mid.shape[2]
    depth = rows + 2 * HALO
    pieces = cols // LANES
    left_on = jnp.where(block_id > 0, 1.0, 0.0)
    right_on = jnp.where((block_id + 1) * cols < total_cols, 1.0, 0.0)
    for part, left, right, start, count in (
        (up, up_l, up_r, 0, HALO),
        (mid, mid_l, mid_r, HALO, rows),
        (dn, dn_l, dn_r, HALO + rows, HALO),
    ):
        for source, col, wide, scale in (
            (left, 0, LANES, left_on),
            (part, LANES, cols, None),
            (right, LANES + cols, LANES, right_on),
        ):
            values = source[0]
            if scale is not None:
                values = values * scale
            high, low = split(values)
            stacked[start : start + count, col : col + wide] = high
            stacked[depth + start : depth + start + count, col : col + wide] = high
            stacked[2 * depth + start : 2 * depth + start + count, col : col + wide] = low
    vertical = jnp.dot(down[0], stacked[...], preferred_element_type=jnp.float32)
    high, low = split(vertical)
    row_id = tile_id * rows + lax.broadcasted_iota(jnp.int32, (rows, LANES), 0)
    y = 2.0 * row_id.astype(jnp.float32) / (total_rows - 1) - 1.0
    matched = [None] * pieces
    for basis_id in range(BASES):
        here = slice(basis_id * rows, (basis_id + 1) * rows)
        windows = [
            part[here, LANES * n : LANES * (n + 3)] for part in (high, low) for n in range(pieces)
        ]
        smooth = jnp.dot(
            jnp.concatenate(windows, axis=0), across[0, basis_id], preferred_element_type=jnp.float32
        )
        c = [coef[visit, basis_id, k] for k in range(6)]
        flat = c[0] + y * (c[2] + y * c[5])
        slope = c[1] + y * c[4]
        for n in range(pieces):
            top = smooth[rows * n : rows * (n + 1)]
            low_part = smooth[rows * (pieces + n) : rows * (pieces + n + 1), 0:LANES]
            value = top[:, 0:LANES] + (top[:, LANES:] + low_part)
            col_id = block_id * cols + LANES * n + lax.broadcasted_iota(jnp.int32, (rows, LANES), 1)
            x = 2.0 * col_id.astype(jnp.float32) / (total_cols - 1) - 1.0
            term = (flat + x * (slope + x * c[3])) * value
            matched[n] = term if basis_id == 0 else matched[n] + term
    for n in range(pieces):
        out[0, 0, :, LANES * n : LANES * (n + 1)] = matched[n]
    out[1, 0] = jnp.where(usable[0] > 0, 1.0 / variance[0], 0.0)


def match(where, cols, total_rows, exposure, above, below, variance, usable, down, across, coef):
    visits, rows, total_cols = exposure.shape
    per_block = cols // LANES
    last = total_cols // LANES - 1

    def main(count):
        return pl.BlockSpec((1, count, cols), lambda v, w: (v, 0, w[0]))

    def left(count):
        return pl.BlockSpec(
            (1, count, LANES), lambda v, w: (v, 0, jnp.maximum(w[0] * per_block - 1, 0))
        )

    def right(count):
        return pl.BlockSpec(
            (1, count, LANES), lambda v, w: (v, 0, jnp.minimum((w[0] + 1) * per_block, last))
        )

    def around(count):
        return [main(count), left(count), right(count)]

    depth = rows + 2 * HALO
    return pl.pallas_call(
        functools.partial(match_kernel, total_rows, total_cols),
        grid_spec=pltpu.PrefetchScalarGridSpec(
            num_scalar_prefetch=1,
            grid=(visits,),
            in_specs=around(rows) + around(HALO) + around(HALO)
            + [
                main(rows),
                main(rows),
                pl.BlockSpec((1,) + down.shape[1:], lambda v, w: (v, 0, 0)),
                pl.BlockSpec((1,) + across.shape[1:], lambda v, w: (v, 0, 0, 0)),
                pl.BlockSpec(memory_space=pltpu.SMEM),
            ],
            out_specs=pl.BlockSpec((2, 1, rows, cols), lambda v, w: (0, v, 0, 0)),
            scratch_shapes=[pltpu.VMEM((3 * depth, cols + 2 * LANES), jnp.bfloat16)],
        ),
        out_shape=jax.ShapeDtypeStruct((2, visits, rows, cols), jnp.float32),
        name="match_block",
        cost_estimate=pl.CostEstimate(
            flops=visits * cols * 1000000,
            bytes_accessed=visits * rows * cols * 40,
            transcendentals=0,
        ),
    )(
        where, exposure, exposure, exposure, above, above, above, below, below, below,
        variance, usable, down, across, coef,
    )


def merge_kernel(*refs):
    *records, out = refs
    rows, cols = out.shape
    visits = records[0].shape[1]
    lanes = pl.ds
    for r in range(0, rows, 8):
        for c in range(0, cols, LANES):
            at = (slice(r, r + 8), slice(c, c + LANES))
            low = [jnp.full((8, LANES), big_value, jnp.float32)] * 3
            high = [jnp.full((8, LANES), -big_value, jnp.float32)] * 3
            for record in records:
                for v in range(visits):
                    value = record[(0, v) + at]
                    on = record[(1, v) + at] > 0.0
                    a = jnp.where(on, value, big_value)
                    b = jnp.where(on, value, -big_value)
                    a1 = jnp.maximum(low[0], a)
                    a2 = jnp.maximum(low[1], a1)
                    low = [jnp.minimum(low[0], a), jnp.minimum(low[1], a1), jnp.minimum(low[2], a2)]
                    b1 = jnp.minimum(high[0], b)
                    b2 = jnp.minimum(high[1], b1)
                    high = [jnp.maximum(high[0], b), jnp.maximum(high[1], b1), jnp.maximum(high[2], b2)]
            numer = jnp.zeros((8, LANES), jnp.float32)
            denom = jnp.zeros((8, LANES), jnp.float32)
            for record in records:
                for v in range(visits):
                    weight = record[(1, v) + at]
                    numer = numer + weight * jnp.clip(record[(0, v) + at], low[2], high[2])
                    denom = denom + weight
            out[at] = numer / denom


def merge(records):
    _, visits, rows, cols = records[0].shape
    wide = min(cols, 2 * LANES)
    spec = pl.BlockSpec((2, visits, rows, wide), lambda i: (0, 0, 0, i))
    return pl.pallas_call(
        merge_kernel,
        grid=(cols // wide,),
        in_specs=[spec] * len(records),
        out_specs=pl.BlockSpec((rows, wide), lambda i: (0, i)),
        out_shape=jax.ShapeDtypeStruct((rows, cols), jnp.float32),
        name="merge_visits",
    )(*records)


def assemble_kernel(where_ref, *refs):
    *blocks, out = refs
    for i, block in enumerate(blocks):
        @pl.when(pl.program_id(0) == i)
        def _():
            out[...] = block[...]


def assemble(where, blocks):
    rows, cols = blocks[0].shape
    count = len(blocks)
    return pl.pallas_call(
        assemble_kernel,
        grid_spec=pltpu.PrefetchScalarGridSpec(
            num_scalar_prefetch=1,
            grid=(count,),
            in_specs=[pl.BlockSpec((rows, cols), lambda i, w: (0, 0))] * count,
            out_specs=pl.BlockSpec((rows, cols), lambda i, w: (0, w[i])),
        ),
        out_shape=jax.ShapeDtypeStruct((rows, cols * count), jnp.float32),
        name="place_blocks",
    )(where, *blocks)


def per_device(exposure, variance, usable, basis_width, spatial_coef):
    visits_here, row_count, col_count = exposure.shape
    ranks = lax.axis_size("visit")
    tiles = lax.axis_size("tile")
    me = lax.axis_index("visit")
    tile_id = lax.axis_index("tile")
    cols = col_count // ranks
    ends = tiles - 1
    above = lax.ppermute(
        exposure[:, row_count - HALO :, :], "tile", [(i, i + 1) for i in range(ends)]
    )
    below = lax.ppermute(exposure[:, :HALO, :], "tile", [(i + 1, i) for i in range(ends)])
    down, across = prep(basis_width, row_count)

    def block(k):
        where = jnp.stack([lax.rem(me + k, ranks), tile_id]).astype(jnp.int32)
        return match(
            where, cols, row_count * tiles, exposure, above, below, variance, usable,
            down, across, spatial_coef,
        )

    def shift(array, k):
        return lax.ppermute(array, "visit", [(i, (i + k) % ranks) for i in range(ranks)])

    received = [shift(block(k), k) for k in range(1, ranks)]
    mine = merge([block(0)] + received)
    blocks = [mine] + [shift(mine, k) for k in range(1, ranks)]
    where = lax.rem(me - jnp.arange(ranks, dtype=jnp.int32) + ranks, ranks)
    return assemble(where, blocks)


def solution(mesh):
    in_specs = (
        P("visit", ("patch", "tile"), None),
        P("visit", ("patch", "tile"), None),
        P("visit", ("patch", "tile"), None),
        P(("patch", "visit"), None),
        P(("patch", "visit"), None, None),
    )
    out_specs = P(("patch", "tile"), None)
    return jax.shard_map(
        per_device, mesh=mesh, in_specs=in_specs, out_specs=out_specs, check_vma=False
    )
```

time: 457 us -> 143 us (0.31)
  waiting for transfers between devices: 317 us -> 57.3 us
  matrix products: 40 us -> 0 us
  Pallas kernels: 0 us -> 38.8 us
  local copies, waits for them, and re-layouts: 43.9 us -> 7.92 us
  other arithmetic: 36.5 us -> 3.03 us
  starting transfers between devices: 4.87 us -> 35.1 us
  between operations: 13.7 us -> 0.1 us
    all_gather x6 -> x0, waiting for transfers between devices: 264 us -> none  [combined_all(): everything = jax.tree.map(lambda part: lax.all_gather(part, axis), array)]
    ppermute x2 -> x8, waiting for transfers between devices: 0.01 us -> 57.3 us  [the longest x6 57.3 us: shift(): lax.ppermute(array, 'visit', [(i, (i + k) % ranks) for i in range(ranks)])]
    psum x1 -> x0, waiting for transfers between devices: 50.9 us -> none  [per_device(): numer_all, denom_all = lax.psum((numer, denom), 'visit')]
    dot_general x3 -> x0, matrix products: 40 us -> none  [the longest x1 20 us: per_device(): jnp.einsum('vbrnk,vbkj->vbrnj', stacked, across_mats, precision=lax.Preci...]
    pallas_call x0 -> x7, Pallas kernels: none -> 38.8 us  [the longest x4 27.6 us: match(): pl.pallas_call(functools.partial(match_kernel, total_rows, total_cols), g...]
    ppermute x2 -> x8, starting transfers between devices: 4.63 us -> 35.1 us  [the longest x6 30.7 us: shift(): lax.ppermute(array, 'visit', [(i, (i + k) % ranks) for i in range(ranks)])]
    max x5 -> x0, other arithmetic: 15.3 us -> none  [the longest x4 14.1 us: merge_records(): jnp.maximum(jnp.maximum(first[5], second[5]), jnp.maximum(jnp.minimum(fir...]
    another operation x6 -> x0, local copies, waits for them, and re-layouts: 10.4 us -> none  [per_device(): jnp.stack([jnp.ones((row_count, col_count), jnp.float32), xcoord, ycoord,...]
  transfers between devices with their start and end apart: 9 -> 8, of which waited for: 7 -> 3; matrix products, arithmetic and copies ran while one was open for 8% -> 3% of each run, Pallas kernels for 0% -> 17%
where the time goes in v1:
time: 143 us; the launch traced here: 142 us
  waiting for transfers between devices  57.3 us (40%)
  Pallas kernels  38.8 us (27%)
  starting transfers between devices  35.1 us (25%)
  local copies, waits for them, and re-layouts  7.92 us (6%)
  other arithmetic  3.03 us (2%)
    ppermute x6, waiting for transfers between devices, shift(): lax.ppermute(array, 'visit', [(i, (i + k) % ranks) for i in range(ranks)])  57.3 us
    ppermute x6, starting transfers between devices, shift(): lax.ppermute(array, 'visit', [(i, (i + k) % ranks) for i in range(ranks)])  30.7 us
    pallas_call x4, Pallas kernels, match(): pl.pallas_call(functools.partial(match_kernel, total_rows, total_cols), g...  27.6 us
    unnamed x19, local copies, waits for them, and re-layouts  5.16 us
    pallas_call x1, Pallas kernels, merge(): pl.pallas_call(merge_kernel, grid=(cols // wide,), in_specs=[spec] * len(...  4.33 us
    pallas_call x1, Pallas kernels, prep(): pl.pallas_call(functools.partial(prep_kernel, rows), grid=(visits,), in_s...  3.73 us
    pallas_call x1, Pallas kernels, assemble(): pl.pallas_call(assemble_kernel, grid_spec=pltpu.PrefetchScalarGridSpec(nu...  3.18 us
    ppermute x1, starting transfers between devices, per_device(): lax.ppermute(exposure[:, row_count - HALO:, :], 'tile', [(i, i + 1) for i...  3.1 us
  transfers between devices with their start and end apart: 8, of which 3 were waited for; matrix products, arithmetic and copies ran while one was open for 3% of the time, Pallas kernels for 17%

profile of v1, /device:TPU:0, one launch (start us, length us, event | category | flops | bytes accessed | tf_op | source)
XLA Modules:
  0.0 142.3 jit_solution(13495453121778529430)
XLA Ops:
  0.0 0.0 copy-start.8
  0.0 2.8 %fusion.1 = (f32[4,16,4096]{2,1,0:T(8,128)}, f32[4,16,4096]{2,1,0:T(8,128)S(1)}) fusion(f32[4,32,4096]{2,1,0:T(8,128)} %mid_r.7), kind=kLoop, calls=%fused_computation.7 | loop fusion | bytes 4194304 | tf_op jit(solution)/shard_map/slice | solution.py:264
  2.8 1.3 collective-permute-start.1
  4.0 3.1 %collective-permute-start = (f32[4,16,4096]{2,1,0:T(8,128)S(1)}, f32[4,16,4096]{2,1,0:T(8,128)S(1)}, u32[]{:S(2)}, u32[]{:S(2)}) collective-permute-start(f32[4,16,4096]{2,1,0:T(8,128)S(1)} %get-tuple-element.10), channel_id=1, source_target_pairs={{0,1},{1,2},{2,3},{4,5},{5,6},{6,7},{8,9},{9,10},{10,11},{12,13},{... | collective-permute-start | bytes 3145736 | tf_op jit(solution)/shard_map/ppermute | solution.py:261
  7.2 0.0 copy-done.8
  7.2 0.6 copy.6.coef
  7.8 3.7 %band_matrices.1 = (bf16[4,96,192]{2,1,0:T(8,128)(2,1)}, bf16[4,3,384,256]{3,2,1,0:T(8,128)(2,1)}) custom-call(f32[4,3]{1,0:T(4,128)} %width_ref.1), custom_call_target="tpu_custom_call" | custom-call | tf_op jit(solution)/shard_map/band_matrices/pallas_call | solution.py:57
  11.5 0.7 pad_add_fusion.1.where_ref
  12.2 0.6 pad_add_fusion.2.where_ref
  12.8 0.6 pad_add_fusion.3.where_ref
  13.4 0.0 collective-permute-done.1.dn.dn_l.dn_r
  13.4 0.0 copy-start
  13.4 0.0 collective-permute-done.up.up_l.up_r
  13.4 0.0 copy-start.1
  13.4 0.9 copy-done
  14.4 0.4 copy-done.1
  14.7 6.9 %match_block.5 = f32[2,4,32,1024]{3,2,1,0:T(8,128)} custom-call(s32[2]{0:T(128)} %pad_add_fusion.1.where_ref, f32[4,32,4096]{2,1,0:T(8,128)} %mid_r.7, f32[4,32,4096]{2,1,0:T(8,128)} %mid_r.7, f32[4,32,4096]{2,1,0:T(8,128)} %mid_r.7, f32[4,16,4096]{2,1,0:T(8,128)} %copy-done.1, f32[4,16,4096]{2,1,0:T(8,128)} %copy-done.1, f32[4,16,4096]{2,1,0:T(8,128)} %copy-done.1, ...), custom_call_target="tpu_custom_call" | custom-call | flops 4096000000 | bytes 5242880 | tf_op jit(solution)/shard_map/match_block/pallas_call | solution.py:154
  21.6 3.1 %collective-permute-start.2 = (f32[2,4,32,1024]{3,2,1,0:T(8,128)}, f32[2,4,32,1024]{3,2,1,0:T(8,128)S(1)}, u32[]{:S(2)}, u32[]{:S(2)}) collective-permute-start(f32[2,4,32,1024]{3,2,1,0:T(8,128)} %match_block.5), channel_id=1, source_target_pairs={{0,4},{4,8},{8,12},{12,0},{1,5},{5,9},{9,13},{13,1},{2,6},{6,10},{... | collective-permute-start | bytes 3145736 | tf_op jit(solution)/shard_map/ppermute | solution.py:275
  24.7 6.9 %match_block.6 = f32[2,4,32,1024]{3,2,1,0:T(8,128)} custom-call(s32[2]{0:T(128)} %pad_add_fusion.2.where_ref, f32[4,32,4096]{2,1,0:T(8,128)} %mid_r.7, f32[4,32,4096]{2,1,0:T(8,128)} %mid_r.7, f32[4,32,4096]{2,1,0:T(8,128)} %mid_r.7, f32[4,16,4096]{2,1,0:T(8,128)} %copy-done.1, f32[4,16,4096]{2,1,0:T(8,128)} %copy-done.1, f32[4,16,4096]{2,1,0:T(8,128)} %copy-done.1, ...), custom_call_target="tpu_custom_call" | custom-call | flops 4096000000 | bytes 5242880 | tf_op jit(solution)/shard_map/match_block/pallas_call | solution.py:154
  31.6 2.6 %collective-permute-start.3 = (f32[2,4,32,1024]{3,2,1,0:T(8,128)}, f32[2,4,32,1024]{3,2,1,0:T(8,128)S(1)}, u32[]{:S(2)}, u32[]{:S(2)}) collective-permute-start(f32[2,4,32,1024]{3,2,1,0:T(8,128)} %match_block.6), channel_id=1, source_target_pairs={{0,8},{4,12},{8,0},{12,4},{1,9},{5,13},{9,1},{13,5},{2,10},{6,14},... | collective-permute-start | bytes 3145736 | tf_op jit(solution)/shard_map/ppermute | solution.py:275
  34.3 6.9 %match_block.7 = f32[2,4,32,1024]{3,2,1,0:T(8,128)} custom-call(s32[2]{0:T(128)} %pad_add_fusion.3.where_ref, f32[4,32,4096]{2,1,0:T(8,128)} %mid_r.7, f32[4,32,4096]{2,1,0:T(8,128)} %mid_r.7, f32[4,32,4096]{2,1,0:T(8,128)} %mid_r.7, f32[4,16,4096]{2,1,0:T(8,128)} %copy-done.1, f32[4,16,4096]{2,1,0:T(8,128)} %copy-done.1, f32[4,16,4096]{2,1,0:T(8,128)} %copy-done.1, ...), custom_call_target="tpu_custom_call" | custom-call | flops 4096000000 | bytes 5242880 | tf_op jit(solution)/shard_map/match_block/pallas_call | solution.py:154
  41.2 1.4 collective-permute-start.4
  42.6 0.6 pad_add_fusion.where_ref
  43.2 6.9 %match_block.4.refs_0_ = f32[2,4,32,1024]{3,2,1,0:T(8,128)} custom-call(s32[2]{0:T(128)} %pad_add_fusion.where_ref, f32[4,32,4096]{2,1,0:T(8,128)} %mid_r.7, f32[4,32,4096]{2,1,0:T(8,128)} %mid_r.7, f32[4,32,4096]{2,1,0:T(8,128)} %mid_r.7, f32[4,16,4096]{2,1,0:T(8,128)} %copy-done.1, f32[4,16,4096]{2,1,0:T(8,128)} %copy-done.1, f32[4,16,4096]{2,1,0:T(8,128)} %copy-done.1, ...), custom_call_target="tpu_custom_call" | custom-call | flops 4096000000 | bytes 5242880 | tf_op jit(solution)/shard_map/match_block/pallas_call | solution.py:154
  50.1 0.0 collective-permute-done.2.refs_1_
  50.1 0.0 copy-start.2
  50.1 45.7 %collective-permute-done.3.refs_2_ = f32[2,4,32,1024]{3,2,1,0:T(8,128)S(1)} collective-permute-done((f32[2,4,32,1024]{3,2,1,0:T(8,128)}, f32[2,4,32,1024]{3,2,1,0:T(8,128)S(1)}, u32[]{:S(2)}, u32[]{:S(2)}) %collective-permute-start.3) | collective-permute-done | bytes 1048608 | tf_op jit(solution)/shard_map/ppermute | solution.py:275
  95.8 0.0 copy-start.3
  95.8 0.0 collective-permute-done.4.refs_3_
  95.8 0.0 copy-done.2
  95.8 0.9 copy-done.3
  96.8 0.0 copy-start.4
  96.8 1.0 copy-done.4
  97.7 4.3 %merge_visits.1.refs_0_ = f32[32,1024]{1,0:T(8,128)} custom-call(f32[2,4,32,1024]{3,2,1,0:T(8,128)} %match_block.4.refs_0_, f32[2,4,32,1024]{3,2,1,0:T(8,128)} %copy-done.2, f32[2,4,32,1024]{3,2,1,0:T(8,128)} %copy-done.3, f32[2,4,32,1024]{3,2,1,0:T(8,128)} %copy-done.4), custom_call_target="tpu_custom_call" | custom-call | tf_op jit(solution)/shard_map/merge_visits/pallas_call | solution.py:219
  102.1 19.3 %collective-permute-start.7 = (f32[32,1024]{1,0:T(8,128)}, f32[32,1024]{1,0:T(8,128)S(1)}, u32[]{:S(2)}, u32[]{:S(2)}) collective-permute-start(f32[32,1024]{1,0:T(8,128)} %merge_visits.1.refs_0_), channel_id=1, source_target_pairs={{0,12},{4,0},{8,4},{12,8},{1,13},{5,1},{9,5},{13,9},{2,14},{6,2},{... | collective-permute-start | bytes 393224 | tf_op jit(solution)/shard_map/ppermute | solution.py:275
  121.3 4.3 %collective-permute-start.6 = (f32[32,1024]{1,0:T(8,128)}, f32[32,1024]{1,0:T(8,128)S(1)}, u32[]{:S(2)}, u32[]{:S(2)}) collective-permute-start(f32[32,1024]{1,0:T(8,128)} %merge_visits.1.refs_0_), channel_id=1, source_target_pairs={{0,8},{4,12},{8,0},{12,4},{1,9},{5,13},{9,1},{13,5},{2,10},{6,14},... | collective-permute-start | bytes 393224 | tf_op jit(solution)/shard_map/ppermute | solution.py:275
  125.6 0.0 collective-permute-start.5
  125.6 0.5 compare_select_fusion.where_ref
  126.2 2.0 %collective-permute-done.7.refs_3_ = f32[32,1024]{1,0:T(8,128)S(1)} collective-permute-done((f32[32,1024]{1,0:T(8,128)}, f32[32,1024]{1,0:T(8,128)S(1)}, u32[]{:S(2)}, u32[]{:S(2)}) %collective-permute-start.7) | collective-permute-done | bytes 131104 | tf_op jit(solution)/shard_map/ppermute | solution.py:275
  128.2 0.0 copy-start.5
  128.2 9.6 %collective-permute-done.6.refs_2_ = f32[32,1024]{1,0:T(8,128)S(1)} collective-permute-done((f32[32,1024]{1,0:T(8,128)}, f32[32,1024]{1,0:T(8,128)S(1)}, u32[]{:S(2)}, u32[]{:S(2)}) %collective-permute-start.6) | collective-permute-done | bytes 131104 | tf_op jit(solution)/shard_map/ppermute | solution.py:275
  137.8 0.0 copy-start.6
  137.8 0.0 collective-permute-done.5.refs_1_
  137.8 0.0 copy-done.5
  137.8 0.6 copy-done.6
  138.4 0.0 copy-start.7
  138.4 0.7 copy-done.7
  139.1 3.2 %place_blocks.1 = f32[32,4096]{1,0:T(8,128)} custom-call(s32[4]{0:T(128)} %compare_select_fusion.where_ref, f32[32,1024]{1,0:T(8,128)} %merge_visits.1.refs_0_, f32[32,1024]{1,0:T(8,128)} %copy-done.7, f32[32,1024]{1,0:T(8,128)} %copy-done.6, f32[32,1024]{1,0:T(8,128)} %copy-done.5), custom_call_target="tpu_custom_call" | custom-call | tf_op jit(solution)/shard_map/place_blocks/pallas_call | solution.py:240
Async XLA Ops:
  0.0 7.2 %copy-start.8 = (f32[4,3,6]{2,0,1:T(4,128)S(1)}, f32[4,3,6]{2,0,1:T(4,128)}, u32[]{:S(2)}) copy-start(f32[4,3,6]{2,0,1:T(4,128)} %param.9) | copy-start | bytes 868
  2.8 10.6 %collective-permute-start.1 = (f32[4,16,4096]{2,1,0:T(8,128)}, f32[4,16,4096]{2,1,0:T(8,128)S(1)}, u32[]{:S(2)}, u32[]{:S(2)}) collective-permute-start(f32[4,16,4096]{2,1,0:T(8,128)} %get-tuple-element.9), channel_id=1, source_target_pairs={{1,0},{2,1},{3,2},{5,4},{6,5},{7,6},{9,8},{10,9},{11,10},{13,12},{... | collective-permute-start | bytes 3145736 | tf_op jit(solution)/shard_map/ppermute | solution.py:264
  4.0 9.4 %collective-permute-start = (f32[4,16,4096]{2,1,0:T(8,128)S(1)}, f32[4,16,4096]{2,1,0:T(8,128)S(1)}, u32[]{:S(2)}, u32[]{:S(2)}) collective-permute-start(f32[4,16,4096]{2,1,0:T(8,128)S(1)} %get-tuple-element.10), channel_id=1, source_target_pairs={{0,1},{1,2},{2,3},{4,5},{5,6},{6,7},{8,9},{9,10},{10,11},{12,13},{... | collective-permute-start | bytes 3145736 | tf_op jit(solution)/shard_map/ppermute | solution.py:261
  13.4 1.0 copy-start
  13.4 1.3 copy-start.1
  21.6 28.5 %collective-permute-start.2 = (f32[2,4,32,1024]{3,2,1,0:T(8,128)}, f32[2,4,32,1024]{3,2,1,0:T(8,128)S(1)}, u32[]{:S(2)}, u32[]{:S(2)}) collective-permute-start(f32[2,4,32,1024]{3,2,1,0:T(8,128)} %match_block.5), channel_id=1, source_target_pairs={{0,4},{4,8},{8,12},{12,0},{1,5},{5,9},{9,13},{13,1},{2,6},{6,10},{... | collective-permute-start | bytes 3145736 | tf_op jit(solution)/shard_map/ppermute | solution.py:275
  31.6 64.2 %collective-permute-start.3 = (f32[2,4,32,1024]{3,2,1,0:T(8,128)}, f32[2,4,32,1024]{3,2,1,0:T(8,128)S(1)}, u32[]{:S(2)}, u32[]{:S(2)}) collective-permute-start(f32[2,4,32,1024]{3,2,1,0:T(8,128)} %match_block.6), channel_id=1, source_target_pairs={{0,8},{4,12},{8,0},{12,4},{1,9},{5,13},{9,1},{13,5},{2,10},{6,14},... | collective-permute-start | bytes 3145736 | tf_op jit(solution)/shard_map/ppermute | solution.py:275
  41.2 54.6 %collective-permute-start.4 = (f32[2,4,32,1024]{3,2,1,0:T(8,128)}, f32[2,4,32,1024]{3,2,1,0:T(8,128)S(1)}, u32[]{:S(2)}, u32[]{:S(2)}) collective-permute-start(f32[2,4,32,1024]{3,2,1,0:T(8,128)} %match_block.7), channel_id=1, source_target_pairs={{0,12},{4,0},{8,4},{12,8},{1,13},{5,1},{9,5},{13,9},{2,14},{6,2},{... | collective-permute-start | bytes 3145736 | tf_op jit(solution)/shard_map/ppermute | solution.py:275
  50.1 45.7 %copy-start.2 = (f32[2,4,32,1024]{3,2,1,0:T(8,128)}, f32[2,4,32,1024]{3,2,1,0:T(8,128)S(1)}, u32[]{:S(2)}) copy-start(f32[2,4,32,1024]{3,2,1,0:T(8,128)S(1)} %collective-permute-done.2.refs_1_) | copy-start | bytes 3145732
  95.8 1.0 copy-start.3
  96.8 1.0 copy-start.4
  102.1 26.1 %collective-permute-start.7 = (f32[32,1024]{1,0:T(8,128)}, f32[32,1024]{1,0:T(8,128)S(1)}, u32[]{:S(2)}, u32[]{:S(2)}) collective-permute-start(f32[32,1024]{1,0:T(8,128)} %merge_visits.1.refs_0_), channel_id=1, source_target_pairs={{0,12},{4,0},{8,4},{12,8},{1,13},{5,1},{9,5},{13,9},{2,14},{6,2},{... | collective-permute-start | bytes 393224 | tf_op jit(solution)/shard_map/ppermute | solution.py:275
  121.3 16.4 %collective-permute-start.6 = (f32[32,1024]{1,0:T(8,128)}, f32[32,1024]{1,0:T(8,128)S(1)}, u32[]{:S(2)}, u32[]{:S(2)}) collective-permute-start(f32[32,1024]{1,0:T(8,128)} %merge_visits.1.refs_0_), channel_id=1, source_target_pairs={{0,8},{4,12},{8,0},{12,4},{1,9},{5,13},{9,1},{13,5},{2,10},{6,14},... | collective-permute-start | bytes 393224 | tf_op jit(solution)/shard_map/ppermute | solution.py:275
  125.6 12.1 %collective-permute-start.5 = (f32[32,1024]{1,0:T(8,128)}, f32[32,1024]{1,0:T(8,128)S(1)}, u32[]{:S(2)}, u32[]{:S(2)}) collective-permute-start(f32[32,1024]{1,0:T(8,128)} %merge_visits.1.refs_0_), channel_id=1, source_target_pairs={{0,4},{4,8},{8,12},{12,0},{1,5},{5,9},{9,13},{13,1},{2,6},{6,10},{... | collective-permute-start | bytes 393224 | tf_op jit(solution)/shard_map/ppermute | solution.py:275
  128.2 9.6 %copy-start.5 = (f32[32,1024]{1,0:T(8,128)}, f32[32,1024]{1,0:T(8,128)S(1)}, u32[]{:S(2)}) copy-start(f32[32,1024]{1,0:T(8,128)S(1)} %collective-permute-done.7.refs_3_) | copy-start | bytes 393220
  137.8 0.7 copy-start.6
  138.4 0.7 copy-start.7
